TPU v7x, 256 devices: a whole 4x4x8 slice. The times are simulated.
256 devices in a mesh: dp: 8 (over z_hi, x), expert: 32 (over z_lo, y, core).
Axes of the slice: x: 4, y: 4, z: 8 (z_hi: 2, z_lo: 4; z = z_hi * 4 + z_lo), core: 2. Of those that a mesh axis runs over, the one named last changes fastest.
Arguments:
- tokens: bfloat16 [32768, 3584], P(('dp', 'expert')), may hold values from -6 to 6
- cotangent: bfloat16 [32768, 3584], P(('dp', 'expert')), may hold values from -0.09375 to 0.09375
- expert_ids: int32 [32768, 8], P(('dp', 'expert')), may hold values from 0 to 255, all different within a row; in each aligned block of 128 rows (0 to 127, 128 to 255, ...) at most 6 rows name the same one
- gates: bfloat16 [32768, 8], P(('dp', 'expert')), may hold values from 0.049804688 to 1
- swap_flags: int32 [16], replicated, may hold values 0 or 1
- gate_w: bfloat16 [32, 3584, 1024], P('expert', None, 'dp'), may hold values from -0.09375 to 0.09375
- up_w: bfloat16 [32, 3584, 1024], P('expert', None, 'dp'), may hold values from -0.09375 to 0.09375
- down_w: bfloat16 [32, 1024, 3584], P('expert', 'dp'), may hold values from -0.1875 to 0.1875
Outputs:
- grad_gate_w: bfloat16 [32, 3584, 1024], P('expert', None, 'dp')
- grad_up_w: bfloat16 [32, 3584, 1024], P('expert', None, 'dp')
- grad_down_w: bfloat16 [32, 1024, 3584], P('expert', 'dp')
- score_grad: float32 [32768, 8], P(('dp', 'expert'))
Inputs may be any that keep to these rules, and one draw needn't show every extreme that they name: `expert_ids`: among the 128 rows of one device no expert is named more than 6 times, a bound that some block reaches; the numbers of one row differ. `swap_flags`: 1 means that slots s and s + 16 trade their experts.
All inputs are finite; a program needn't handle non-finite values.
Results may differ from a plain program's by a relative error of at most 0.011.
Values may be sent and summed in bfloat16 or wider, within the bound.
A program may use at most 128 MiB of HBM per device.

v0:
```python
import jax
import jax.numpy as jnp
from jax import lax
from jax.sharding import PartitionSpec as P

CAP = 6


def partner(block, axis, stride):
    count = lax.axis_size(axis)
    route = []
    for low in range(count):
        high = low | 1 << stride
        if high != low and high < count:
            route += [(low, high), (high, low)]
    return lax.ppermute(block, axis, route)


def body(tokens, cotangent, expert_ids, gates, swap_flags, gate_w, up_w, down_w):
    axis_len = lax.axis_size("expert")
    half_axis = axis_len // 2
    pair_bit = axis_len.bit_length() - 2
    own_slot = lax.axis_index("expert")
    tok_count = tokens.shape[0]
    top_count = expert_ids.shape[1]
    width = tokens.shape[1]
    flat_ids = expert_ids.reshape(-1)
    choice_count = flat_ids.shape[0]
    valid = flat_ids < axis_len
    pair_index = jnp.arange(half_axis, dtype=jnp.int32)
    flag_of = jnp.sum(
        jnp.where((flat_ids % half_axis)[:, None] == pair_index[None, :], swap_flags[None, :], 0),
        axis=1,
    )
    own_flag = jnp.sum(jnp.where(pair_index == own_slot % half_axis, swap_flags, 0))
    target = jnp.where(flag_of == 1, jnp.bitwise_xor(flat_ids, half_axis), flat_ids)
    target = jnp.where(valid, target, 0)
    onehot = jnp.where(
        (target[:, None] == jnp.arange(axis_len, dtype=jnp.int32)[None, :]) & valid[:, None], 1, 0
    ).astype(jnp.int32)
    ranks = jnp.sum(jnp.cumsum(onehot, axis=0) * onehot, axis=1) - 1
    slot_count = axis_len * CAP
    slots = jnp.where(valid, target * CAP + ranks, slot_count)
    source = (
        jnp.full((slot_count,), choice_count, jnp.int32)
        .at[slots]
        .set(jnp.arange(choice_count, dtype=jnp.int32), mode="drop")
    )
    token_index = source // top_count
    padded_x = jnp.concatenate([tokens, jnp.zeros((1, width), tokens.dtype)], axis=0)
    padded_dy = jnp.concatenate([cotangent, jnp.zeros((1, width), cotangent.dtype)], axis=0)
    padded_g = jnp.concatenate([gates.reshape(-1), jnp.zeros((1,), gates.dtype)], axis=0)
    send_x = padded_x[token_index].reshape(axis_len, CAP, width)
    send_dy = padded_dy[token_index].reshape(axis_len, CAP, width)
    send_g = padded_g[source].reshape(axis_len, CAP)
    recv_x, recv_dy, recv_g = (
        lax.all_to_all(send_x, "expert", split_axis=0, concat_axis=0, tiled=True),
        lax.all_to_all(send_dy, "expert", split_axis=0, concat_axis=0, tiled=True),
        lax.all_to_all(send_g, "expert", split_axis=0, concat_axis=0, tiled=True),
    )
    w_gate = gate_w[0]
    w_up = up_w[0]
    w_down = down_w[0]
    other_gate, other_up, other_down = partner((gate_w, up_w, down_w), "expert", pair_bit)
    taken = own_flag == 1
    w_gate = jnp.where(taken, other_gate[0], w_gate)
    w_up = jnp.where(taken, other_up[0], w_up)
    w_down = jnp.where(taken, other_down[0], w_down)
    contract = (((0,), (0,)), ((), ()))
    part_x = lax.all_gather(recv_x, "dp", axis=0, tiled=True)
    part_dy = lax.all_gather(recv_dy, "dp", axis=0, tiled=True)
    part_g = lax.all_gather(recv_g, "dp", axis=0, tiled=True)
    block_count = part_x.shape[0]
    row_x = part_x.reshape(-1, width)
    row_dy = part_dy.reshape(-1, width)
    row_g = part_g.reshape(-1, 1)
    pre_gate = jnp.dot(row_x, w_gate, preferred_element_type=jnp.float32)
    pre_up = jnp.dot(row_x, w_up, preferred_element_type=jnp.float32)
    sigma = jax.nn.sigmoid(pre_gate)
    active = pre_gate * sigma
    hidden = (active * pre_up).astype(jnp.bfloat16)
    back = lax.dot_general(
        row_dy, w_down, (((1,), (1,)), ((), ())), preferred_element_type=jnp.float32
    )
    score = jnp.sum(hidden.astype(jnp.float32) * back, axis=1)
    scaled = row_dy * row_g
    d_hidden = row_g.astype(jnp.float32) * back
    d_gate = (d_hidden * pre_up * sigma * (1.0 + pre_gate * (1.0 - sigma))).astype(jnp.bfloat16)
    d_up = (d_hidden * active).astype(jnp.bfloat16)
    grad_gate = lax.dot_general(row_x, d_gate, contract, preferred_element_type=jnp.float32)
    grad_up = lax.dot_general(row_x, d_up, contract, preferred_element_type=jnp.float32)
    grad_down = lax.dot_general(hidden, scaled, contract, preferred_element_type=jnp.float32)
    scores = score.reshape(block_count, CAP)
    grad_gate, grad_up, grad_down, scores = (grad_gate, grad_up, grad_down, scores)
    summed = lax.psum(scores, "dp")
    own_scores = lax.dynamic_slice_in_dim(summed, lax.axis_index("dp") * axis_len, axis_len, 0)
    returned = lax.all_to_all(own_scores, "expert", split_axis=0, concat_axis=0, tiled=True)
    picked = returned.reshape(-1)[jnp.minimum(slots, slot_count - 1)]
    score_grad = jnp.where(valid, picked, 0.0).reshape(tok_count, top_count)
    out_gate = grad_gate.astype(jnp.bfloat16)[None]
    out_up = grad_up.astype(jnp.bfloat16)[None]
    out_down = grad_down.astype(jnp.bfloat16)[None]
    return (out_gate, out_up, out_down, score_grad)


def solution(mesh):
    placed = (
        P(("dp", "expert"), None),
        P(("dp", "expert"), None),
        P(("dp", "expert"), None),
        P(("dp", "expert"), None),
        P(),
        P("expert", None, "dp"),
        P("expert", None, "dp"),
        P("expert", "dp", None),
    )
    return jax.shard_map(
        body,
        mesh=mesh,
        in_specs=placed,
        out_specs=(
            P("expert", None, "dp"),
            P("expert", None, "dp"),
            P("expert", "dp", None),
            P(("dp", "expert"), None),
        ),
        check_vma=False,
    )
```

profile of v0, /device:TPU:1, one launch (start us, length us, event | category | flops | bytes accessed | tf_op | source)
XLA Modules:
  0.0 742.2 jit_solution(1144176695480367231)
XLA Ops:
  7.2 0.8 copy.63
  8.3 0.7 select_reduce_fusion
  9.1 9.0 %reduce-window.6 = s32[32,8,128]{2,1,0:T(8,128)S(1)} reduce-window(s32[32,8,128]{2,1,0:T(8,128)S(1)} %fusion.31, s32[]{:T(128)} %constant.32.clone.1), window={size=1x1x128 pad=0_0x0_0x127_0}, to_apply=%region_1.2 | reduce-window | flops 4161536 | bytes 262148 | tf_op jit(solution)/shard_map/reduce-window
  18.2 0.1 copy.66
  18.7 4.3 scatter_custom_fusion
  23.1 1.2 concatenate.9
  24.3 1.4 gather_fusion
  25.7 0.5 reshape.224
  26.2 54.0 %all_to_all.32 = bf16[32,6,3584]{2,1,0:T(8,128)(2,1)S(1)} all-to-all(bf16[32,6,3584]{2,1,0:T(8,128)(2,1)S(1)} %reshape.224), channel_id=1, replica_groups=mesh['dp'=8,'expert'=32] {'expert'}, dimensions={0} | all-to-all | bytes 2752512 | tf_op jit(solution)/shard_map/all_to_all | solution.py:57
  80.2 1.5 copy.68
  81.8 1.2 concatenate.11
  83.1 1.4 gather_fusion.2
  84.5 0.5 reshape.228
  85.0 78.0 %all_to_all.33 = bf16[32,6,3584]{2,1,0:T(8,128)(2,1)S(1)} all-to-all(bf16[32,6,3584]{2,1,0:T(8,128)(2,1)S(1)} %reshape.228), channel_id=1, replica_groups=mesh['dp'=8,'expert'=32] {'expert'}, dimensions={0} | all-to-all | bytes 2752512 | tf_op jit(solution)/shard_map/all_to_all | solution.py:58
  163.0 1.6 copy.72
  164.5 1.0 collective-permute-start.1
  165.5 1.5 collective-permute-start.2
  167.0 0.9 collective-permute-start
  167.9 0.1 copy.70
  168.0 0.1 reshape.226
  168.1 1.6 gather_fusion.1
  169.7 0.7 all_to_all.27
  170.5 5.8 all-to-all-start.1
  176.3 0.6 fusion.36
  177.6 242.5 %all-to-all-done.1 = bf16[32,1,6]{2,1,0:T(2,128)(2,1)S(1)} async-done(((bf16[32,1,6]{2,1,0:T(2,128)(2,1)}), bf16[32,1,6]{2,1,0:T(2,128)(2,1)S(1)}, u32[]{:S(2)}, u32[]{:S(2)}) %all-to-all-start.1) | async-done | bytes 416 | tf_op jit(solution)/shard_map/all_to_all | solution.py:59
  420.1 43.9 %all-gather = bf16[256,1,6]{2,1,0:T(2,128)(2,1)S(1)} all-gather(bf16[32,1,6]{2,1,0:T(2,128)(2,1)S(1)} %all-to-all-done.1), channel_id=2, replica_groups=mesh['dp'=8,'expert'=32] {'dp'}, dimensions={0}, use_global_device_ids=true | all-gather | bytes 3456 | tf_op jit(solution)/shard_map/all_gather | solution.py:72
  463.9 0.4 reduce
  464.3 0.2 reshape.227
  464.5 13.1 %copy.69 = bf16[256,6,3584]{2,1,0:T(8,128)(2,1)} copy(bf16[256,6,3584]{2,0,1:T(8,128)(2,1)} %all-gather.4.cloned.1.call-done) | data formatting | bytes 22020096 | tf_op jit(solution)/shard_map/all_gather | solution.py:70
  477.6 17.7 %reshape.225 = bf16[1536,3584]{1,0:T(8,128)(2,1)} reshape(bf16[256,6,3584]{2,1,0:T(8,128)(2,1)} %copy.69) | data formatting | bytes 22020096 | tf_op jit(solution)/shard_map/reshape | solution.py:74
  495.3 106.1 %all-gather.6.cloned.1.call-done = bf16[256,6,3584]{2,0,1:T(8,128)(2,1)} async-done(((bf16[32,6,3584]{2,0,1:T(8,128)(2,1)}), bf16[256,6,3584]{2,0,1:T(8,128)(2,1)}) %all-gather.6.cloned.1.call-update) | async-done | bytes 11010064 | tf_op jit(solution)/shard_map/all_gather | solution.py:71
  601.5 13.1 %copy.73 = bf16[256,6,3584]{2,1,0:T(8,128)(2,1)} copy(bf16[256,6,3584]{2,0,1:T(8,128)(2,1)} %all-gather.6.cloned.1.call-done) | data formatting | bytes 22020096 | tf_op jit(solution)/shard_map/all_gather | solution.py:71
  614.5 17.8 %reshape.229 = bf16[1536,3584]{1,0:T(8,128)(2,1)} reshape(bf16[256,6,3584]{2,1,0:T(8,128)(2,1)} %copy.73) | data formatting | bytes 22020096 | tf_op jit(solution)/shard_map/reshape | solution.py:75
  632.4 8.0 %fusion.13 = f32[1536,128]{0,1:T(8,128)S(1)} fusion(bf16[1536,3584]{1,0:T(8,128)(2,1)} %reshape.225, bf16[1,3584,128]{2,1,0:T(8,128)(2,1)S(1)} %collective-permute-done.1, bf16[1,3584,128]{2,1,0:T(8,128)(2,1)S(1)} %copy-done, pred[]{:T(512)S(6)} %eq.85), kind=kOutput, calls=%fused_computation.16 | convolution fusion | flops 1409744896 | bytes 13631489 | tf_op jit(solution)/shard_map/dot_general | solution.py:78
  640.4 8.2 %fusion.11 = f32[1536,128]{0,1:T(8,128)S(1)} fusion(bf16[1536,3584]{1,0:T(8,128)(2,1)} %reshape.225, bf16[1,3584,128]{2,1,0:T(8,128)(2,1)} %collective-permute-done.2, bf16[1,3584,128]{2,1,0:T(8,128)(2,1)} %param.13, pred[]{:T(512)S(6)} %eq.85), kind=kOutput, calls=%fused_computation.14 | convolution fusion | flops 1409744896 | bytes 13631489 | tf_op jit(solution)/shard_map/dot_general | solution.py:77
  648.7 5.7 multiply_reduce_fusion
  654.4 4.0 fusion.7
  658.4 4.3 fusion.6
  662.7 0.1 reshape.230
  662.9 41.4 %psum.7 = f32[256,6]{1,0:T(8,128)S(1)} all-reduce(f32[256,6]{1,0:T(8,128)S(1)} %reshape.230), channel_id=1, replica_groups=mesh['dp'=8,'expert'=32] {'dp'}, use_global_device_ids=true, to_apply=%region_7.8 | all-reduce | flops 1536 | bytes 12288 | tf_op jit(solution)/shard_map/psum | solution.py:95
  704.2 0.6 constant_dynamic-slice_fusion
  704.8 14.3 %all-to-all-start.3 = ((f32[32,1,6]{2,1,0:T(1,128)}), f32[32,1,6]{2,1,0:T(1,128)S(1)}, u32[]{:S(2)}, u32[]{:S(2)}) async-start(f32[32,1,6]{2,1,0:T(1,128)} %bitcast.11), calls=%async_computation.3 | async-start | bytes 32768 | tf_op jit(solution)/shard_map/all_to_all | solution.py:97
  719.2 6.9 fusion.8
  726.1 0.4 all-to-all-done.3
  726.5 0.5 broadcast.262
  727.0 0.7 reduce.4
  727.8 6.8 gather_fusion.3
  734.8 0.6 compare_select_fusion.4
  (59 shorter events, 1.2 us)
Async XLA Ops:
  7.2 457.4 %all-gather.4.cloned.1.call-start = ((), (), s32[]{:S(2)}) async-start(), calls=%async_computation.4 | async-start | bytes 12386304 | tf_op jit(solution)/shard_map/all_gather | solution.py:70
  81.7 519.7 %all-gather.6.cloned.1.call-start = ((), (), s32[]{:S(2)}) async-start(), calls=%async_computation.5 | async-start | bytes 12386304 | tf_op jit(solution)/shard_map/all_gather | solution.py:71
  83.0 84.8 %copy-start.2 = (bf16[128,8]{0,1:T(8,128)(2,1)S(1)}, bf16[128,8]{0,1:T(8,128)(2,1)}, u32[]{:S(2)}) copy-start(bf16[128,8]{0,1:T(8,128)(2,1)} %param.11) | copy-start | bytes 6148
  83.1 93.3 %copy-start.3 = (s32[16]{0:T(128)S(1)}, s32[16]{0:T(128)}, u32[]{:S(2)}) copy-start(s32[16]{0:T(128)} %param.12) | copy-start | bytes 196
  164.5 467.8 %collective-permute-start.1 = (bf16[1,3584,128]{2,1,0:T(8,128)(2,1)}, bf16[1,3584,128]{2,1,0:T(8,128)(2,1)S(1)}, u32[]{:S(2)}, u32[]{:S(2)}) collective-permute-start(bf16[1,3584,128]{2,1,0:T(8,128)(2,1)} %param.14), channel_id=1, source_target_pairs={{0,16},{16,0},{1,17},{17,1},{2,18},{18,2},{3,19},{19,3},{4,20},{20... | collective-permute-start | bytes 2752520 | tf_op jit(solution)/shard_map/ppermute | solution.py:16
  165.5 474.9 %collective-permute-start.2 = (bf16[1,3584,128]{2,1,0:T(8,128)(2,1)}, bf16[1,3584,128]{2,1,0:T(8,128)(2,1)}, u32[]{:S(2)}, u32[]{:S(2)}) collective-permute-start(bf16[1,3584,128]{2,1,0:T(8,128)(2,1)} %param.13), channel_id=1, source_target_pairs={{0,16},{16,0},{1,17},{17,1},{2,18},{18,2},{3,19},{19,3},{4,20},{20... | collective-permute-start | bytes 2752520 | tf_op jit(solution)/shard_map/ppermute | solution.py:16
  167.0 481.6 %collective-permute-start = (bf16[1,128,3584]{2,1,0:T(8,128)(2,1)}, bf16[1,128,3584]{2,1,0:T(8,128)(2,1)}, u32[]{:S(2)}, u32[]{:S(2)}) collective-permute-start(bf16[1,128,3584]{2,1,0:T(8,128)(2,1)} %param.15), channel_id=1, source_target_pairs={{0,16},{16,0},{1,17},{17,1},{2,18},{18,2},{3,19},{19,3},{4,20},{20... | collective-permute-start | bytes 2752520 | tf_op jit(solution)/shard_map/ppermute | solution.py:16
  170.5 249.6 %all-to-all-start.1 = ((bf16[32,1,6]{2,1,0:T(2,128)(2,1)}), bf16[32,1,6]{2,1,0:T(2,128)(2,1)S(1)}, u32[]{:S(2)}, u32[]{:S(2)}) async-start(bf16[32,1,6]{2,1,0:T(2,128)(2,1)} %all_to_all.27), calls=%async_computation.1 | async-start | bytes 32768 | tf_op jit(solution)/shard_map/all_to_all | solution.py:59
  614.5 17.8 %copy-start = (bf16[1,3584,128]{2,1,0:T(8,128)(2,1)S(1)}, bf16[1,3584,128]{2,1,0:T(8,128)(2,1)}, u32[]{:S(2)}) copy-start(bf16[1,3584,128]{2,1,0:T(8,128)(2,1)} %param.14) | copy-start | bytes 2752516
  632.3 16.3 %slice-start.3 = ((s8[11010048]{0:T(1024)(128)(4,1)}), s8[4194304]{0:T(1024)(128)(4,1)S(1)}, s32[]{:S(2)}) async-start(s8[11010048]{0:T(1024)(128)(4,1)} %bitcast.45), calls=%async_computation.9 | async-start | bytes 8388608
  632.3 16.3 %slice-start.4 = ((s8[11010048]{0:T(1024)(128)(4,1)}), s8[4194304]{0:T(1024)(128)(4,1)S(1)}, s32[]{:S(2)}) async-start(s8[11010048]{0:T(1024)(128)(4,1)} %bitcast.45), calls=%async_computation.10 | async-start | bytes 8388608
  640.4 8.3 %slice-start.5 = ((s8[11010048]{0:T(1024)(128)(4,1)}), s8[2621440]{0:T(1024)(128)(4,1)S(1)}, s32[]{:S(2)}) async-start(s8[11010048]{0:T(1024)(128)(4,1)} %bitcast.45), calls=%async_computation.11 | async-start | bytes 5242880
  640.4 14.0 %slice-start = ((s8[11010048]{0:T(1024)(128)(4,1)}), s8[4194304]{0:T(1024)(128)(4,1)S(1)}, s32[]{:S(2)}) async-start(s8[11010048]{0:T(1024)(128)(4,1)} %bitcast.43), calls=%async_computation.6 | async-start | bytes 8388608
  640.4 14.0 %slice-start.1 = ((s8[11010048]{0:T(1024)(128)(4,1)}), s8[2621440]{0:T(1024)(128)(4,1)S(1)}, s32[]{:S(2)}) async-start(s8[11010048]{0:T(1024)(128)(4,1)} %bitcast.43), calls=%async_computation.7 | async-start | bytes 5242880
  648.6 5.8 slice-start.2
  658.4 60.7 %copy-start.4 = (bf16[1536,128]{0,1:T(8,128)(2,1)S(1)}, bf16[1536,128]{0,1:T(8,128)(2,1)}, u32[]{:S(2)}) copy-start(bf16[1536,128]{0,1:T(8,128)(2,1)} %get-tuple-element.23) | copy-start | bytes 1179652
  662.7 72.1 %copy-start.1 = (s32[128,8]{0,1:T(8,128)S(1)}, s32[128,8]{0,1:T(8,128)}, u32[]{:S(2)}) copy-start(s32[128,8]{0,1:T(8,128)} %param.10) | copy-start | bytes 12292
  704.8 21.6 %all-to-all-start.3 = ((f32[32,1,6]{2,1,0:T(1,128)}), f32[32,1,6]{2,1,0:T(1,128)S(1)}, u32[]{:S(2)}, u32[]{:S(2)}) async-start(f32[32,1,6]{2,1,0:T(1,128)} %bitcast.11), calls=%async_computation.3 | async-start | bytes 32768 | tf_op jit(solution)/shard_map/all_to_all | solution.py:97
Sparse Core Ops, SparseCore 0:
  81.9 288.9 all-gather.3
  373.4 228.0 all-gather.5
where the time goes:
time: 744 us; the launch traced here: 742 us
  waiting for transfers between devices  349 us (47%)
  blocking collectives  217 us (29%)
  local copies, waits for them, and re-layouts  87.8 us (12%)
  matrix products  37.1 us (5%)
  starting transfers between devices  23.6 us (3%)
  between operations  15.1 us (2%)
  other arithmetic  12.4 us (2%)
    all_to_all x1, waiting for transfers between devices, body(): lax.all_to_all(send_g, 'expert', split_axis=0, concat_axis=0, tiled=True)  242 us
    all_gather x1, waiting for transfers between devices, body(): part_dy = lax.all_gather(recv_dy, 'dp', axis=0, tiled=True)  106 us
    all_to_all x1, blocking collectives, body(): lax.all_to_all(send_dy, 'expert', split_axis=0, concat_axis=0, tiled=True)  78 us
    all_to_all x1, blocking collectives, body(): lax.all_to_all(send_x, 'expert', split_axis=0, concat_axis=0, tiled=True)  54 us
    all_gather x1, blocking collectives, body(): part_g = lax.all_gather(recv_g, 'dp', axis=0, tiled=True)  43.9 us
    psum x1, blocking collectives, body(): summed = lax.psum(scores, 'dp')  41.4 us
    reshape x1, local copies, waits for them, and re-layouts, body(): row_dy = part_dy.reshape(-1, width)  17.8 us
    reshape x1, local copies, waits for them, and re-layouts, body(): row_x = part_x.reshape(-1, width)  17.7 us
  transfers between devices with their start and end apart: 7, of which 3 were waited for; matrix products, arithmetic and copies ran while one was open for 12% of the time, Pallas kernels for 0%

commit v1 on v0

--- a/solution.py
+++ b/solution.py
@@ -4,6 +4,15 @@
 from jax.sharding import PartitionSpec as P
 
 CAP = 6
+
+
+def _write_pages(x0, unit, peer_axis):
+    long_array = jnp.split(
+        jax.lax.all_gather(jnp.concatenate([unit, x0], 1), peer_axis, axis=0, tiled=True),
+        [unit.shape[1]],
+        1,
+    )
+    return long_array
 
 
 def partner(block, axis, stride):
@@ -67,8 +76,7 @@
     w_up = jnp.where(taken, other_up[0], w_up)
     w_down = jnp.where(taken, other_down[0], w_down)
     contract = (((0,), (0,)), ((), ()))
-    part_x = lax.all_gather(recv_x, "dp", axis=0, tiled=True)
-    part_dy = lax.all_gather(recv_dy, "dp", axis=0, tiled=True)
+    part_x, part_dy = _write_pages(recv_dy, recv_x, "dp")
     part_g = lax.all_gather(recv_g, "dp", axis=0, tiled=True)
     block_count = part_x.shape[0]
     row_x = part_x.reshape(-1, width)

time: 744 us -> 778 us (1.046)
  starting transfers between devices: 23.6 us -> 66.7 us
  waiting for transfers between devices: 349 us -> 323 us
  local copies, waits for them, and re-layouts: 87.8 us -> 102 us
    all_gather x2 -> x1, waiting for transfers between devices: 106 us -> 0.02 us  [_write_pages(): jax.lax.all_gather(jnp.concatenate([unit, x0], 1), peer_axis, axis=0, til...]
    all_gather x1, blocking collectives: 43.9 us -> 123 us  [body(): part_g = lax.all_gather(recv_g, 'dp', axis=0, tiled=True)]
    all_to_all x1 -> x0, blocking collectives: 54 us -> none  [body(): lax.all_to_all(send_x, 'expert', split_axis=0, concat_axis=0, tiled=True)]
    all_to_all x1, waiting for transfers between devices: 242 us -> 288 us  [body(): lax.all_to_all(send_g, 'expert', split_axis=0, concat_axis=0, tiled=True)]
    all_to_all x0 -> x1, waiting for transfers between devices: none -> 35.2 us  [body(): lax.all_to_all(send_x, 'expert', split_axis=0, concat_axis=0, tiled=True)]
    split x0 -> x3, local copies, waits for them, and re-layouts: none -> 35.2 us  [_write_pages(): jnp.split(jax.lax.all_gather(jnp.concatenate([unit, x0], 1), peer_axis, a...]
    all_to_all x1, starting transfers between devices: 14.3 us -> 47.3 us  [body(): lax.all_to_all(own_scores, 'expert', split_axis=0, concat_axis=0, tiled=T...]
    all_to_all x1, blocking collectives: 78 us -> 50.3 us  [body(): lax.all_to_all(send_dy, 'expert', split_axis=0, concat_axis=0, tiled=True)]
  transfers between devices with their start and end apart: 7 -> 7, of which waited for: 3 -> 3; matrix products, arithmetic and copies ran while one was open for 12% -> 13% of each run, Pallas kernels for 0% -> 0%
where the time goes in v1:
time: 778 us; the launch traced here: 776 us
  waiting for transfers between devices  323 us (42%)
  blocking collectives  218 us (28%)
  local copies, waits for them, and re-layouts  102 us (13%)
  starting transfers between devices  66.7 us (9%)
  matrix products  37.2 us (5%)
  between operations  15.1 us (2%)
  other arithmetic  13.6 us (2%)
    all_to_all x1, waiting for transfers between devices, body(): lax.all_to_all(send_g, 'expert', split_axis=0, concat_axis=0, tiled=True)  288 us
    all_gather x1, blocking collectives, body(): part_g = lax.all_gather(recv_g, 'dp', axis=0, tiled=True)  123 us
    all_to_all x1, blocking collectives, body(): lax.all_to_all(send_dy, 'expert', split_axis=0, concat_axis=0, tiled=True)  50.3 us
    all_to_all x1, starting transfers between devices, body(): lax.all_to_all(own_scores, 'expert', split_axis=0, concat_axis=0, tiled=T...  47.3 us
    psum x1, blocking collectives, body(): summed = lax.psum(scores, 'dp')  44.8 us
    all_to_all x1, waiting for transfers between devices, body(): lax.all_to_all(send_x, 'expert', split_axis=0, concat_axis=0, tiled=True)  35.2 us
    split x3, local copies, waits for them, and re-layouts, _write_pages(): jnp.split(jax.lax.all_gather(jnp.concatenate([unit, x0], 1), peer_axis, a...  35.2 us
    reshape x1, local copies, waits for them, and re-layouts, body(): row_x = part_x.reshape(-1, width)  17.7 us
  transfers between devices with their start and end apart: 7, of which 3 were waited for; matrix products, arithmetic and copies ran while one was open for 13% of the time, Pallas kernels for 0%

profile of v1, /device:TPU:1, one launch (start us, length us, event | category | flops | bytes accessed | tf_op | source)
XLA Modules:
  0.0 776.1 jit_solution(10099934362769380648)
XLA Ops:
  7.2 0.8 copy.60
  8.3 0.7 select_reduce_fusion
  9.1 9.0 %reduce-window.6 = s32[32,8,128]{2,1,0:T(8,128)S(1)} reduce-window(s32[32,8,128]{2,1,0:T(8,128)S(1)} %fusion.31, s32[]{:T(128)} %constant.32.clone.1), window={size=1x1x128 pad=0_0x0_0x127_0}, to_apply=%region_1.2 | reduce-window | flops 4161536 | bytes 262148 | tf_op jit(solution)/shard_map/reduce-window
  18.2 0.1 copy.63
  18.7 4.3 scatter_custom_fusion
  23.0 1.2 concatenate.12
  24.3 1.4 gather_fusion
  25.7 1.5 reshape.224
  27.2 10.2 %all-to-all-start = ((bf16[32,6,3584]{2,1,0:T(8,128)(2,1)}), bf16[32,6,3584]{2,1,0:T(8,128)(2,1)S(1)}, u32[]{:S(2)}, u32[]{:S(2)}) async-start(bf16[32,6,3584]{2,1,0:T(8,128)(2,1)} %reshape.224), calls=%async_computation | async-start | bytes 3670016 | tf_op jit(solution)/shard_map/all_to_all | solution.py:66
  37.4 1.2 concatenate.13
  38.7 2.5 gather_fusion.1
  41.2 3.4 reshape.225
  44.7 35.2 %all-to-all-done = bf16[32,6,3584]{2,1,0:T(8,128)(2,1)S(1)} async-done(((bf16[32,6,3584]{2,1,0:T(8,128)(2,1)}), bf16[32,6,3584]{2,1,0:T(8,128)(2,1)S(1)}, u32[]{:S(2)}, u32[]{:S(2)}) %all-to-all-start) | async-done | bytes 1376288 | tf_op jit(solution)/shard_map/all_to_all | solution.py:66
  79.9 50.3 %all_to_all.32 = bf16[32,6,3584]{2,1,0:T(8,128)(2,1)S(1)} all-to-all(bf16[32,6,3584]{2,1,0:T(8,128)(2,1)} %reshape.225), channel_id=1, replica_groups=mesh['dp'=8,'expert'=32] {'expert'}, dimensions={0} | all-to-all | bytes 2752512 | tf_op jit(solution)/shard_map/all_to_all | solution.py:67
  130.2 1.2 pad_maximum_fusion
  131.4 3.0 copy.65
  134.4 1.0 collective-permute-start.1
  135.4 1.5 collective-permute-start.2
  136.9 0.9 collective-permute-start
  137.8 0.1 copy.67
  138.0 1.6 gather_fusion.2
  139.6 0.7 all_to_all.27
  140.4 5.8 all-to-all-start.2
  146.2 0.6 fusion.36
  147.5 287.8 %all-to-all-done.2 = bf16[32,1,6]{2,1,0:T(2,128)(2,1)S(1)} async-done(((bf16[32,1,6]{2,1,0:T(2,128)(2,1)}), bf16[32,1,6]{2,1,0:T(2,128)(2,1)S(1)}, u32[]{:S(2)}, u32[]{:S(2)}) %all-to-all-start.2) | async-done | bytes 416 | tf_op jit(solution)/shard_map/all_to_all | solution.py:68
  435.3 123.2 %all-gather = bf16[256,1,6]{2,1,0:T(2,128)(2,1)S(1)} all-gather(bf16[32,1,6]{2,1,0:T(2,128)(2,1)S(1)} %all-to-all-done.2), channel_id=2, replica_groups=mesh['dp'=8,'expert'=32] {'dp'}, dimensions={0}, use_global_device_ids=true | all-gather | bytes 3456 | tf_op jit(solution)/shard_map/all_gather | solution.py:80
  558.5 0.4 reduce
  558.9 0.2 reshape.228
  559.1 12.0 %fusion.41 = (bf16[256,6,3584]{2,0,1:T(8,128)(2,1)}, bf16[256,6,3584]{2,0,1:T(8,128)(2,1)S(1)}) fusion(bf16[256,12,3584]{2,0,1:T(8,128)(2,1)} %all-gather.3.cloned.1.call-done), kind=kLoop, calls=%fused_computation.82 | loop fusion | bytes 44040192 | tf_op jit(solution)/shard_map/split | solution.py:10
  571.1 10.1 %copy.66 = bf16[256,6,3584]{2,1,0:T(8,128)(2,1)} copy(bf16[256,6,3584]{2,0,1:T(8,128)(2,1)S(1)} %get-tuple-element.27) | data formatting | bytes 22020096 | tf_op jit(solution)/shard_map/split | solution.py:10
  581.2 17.7 %reshape.226 = bf16[1536,3584]{1,0:T(8,128)(2,1)} reshape(bf16[256,6,3584]{2,1,0:T(8,128)(2,1)} %copy.66) | data formatting | bytes 22020096 | tf_op jit(solution)/shard_map/reshape | solution.py:82
  599.0 13.1 %copy.69 = bf16[256,6,3584]{2,1,0:T(8,128)(2,1)} copy(bf16[256,6,3584]{2,0,1:T(8,128)(2,1)} %get-tuple-element.26) | data formatting | bytes 22020096 | tf_op jit(solution)/shard_map/split | solution.py:10
  612.0 17.7 %reshape.229 = bf16[1536,3584]{1,0:T(8,128)(2,1)} reshape(bf16[256,6,3584]{2,1,0:T(8,128)(2,1)} %copy.69) | data formatting | bytes 22020096 | tf_op jit(solution)/shard_map/reshape | solution.py:83
  629.8 8.0 %fusion.13 = f32[1536,128]{0,1:T(8,128)S(1)} fusion(bf16[1536,3584]{1,0:T(8,128)(2,1)} %reshape.226, bf16[1,3584,128]{2,1,0:T(8,128)(2,1)S(1)} %collective-permute-done.1, bf16[1,3584,128]{2,1,0:T(8,128)(2,1)S(1)} %copy-done, pred[]{:T(512)S(6)} %eq.85), kind=kOutput, calls=%fused_computation.17 | convolution fusion | flops 1409744896 | bytes 13631489 | tf_op jit(solution)/shard_map/dot_general | solution.py:86
  637.9 8.2 %fusion.11 = f32[1536,128]{0,1:T(8,128)S(1)} fusion(bf16[1536,3584]{1,0:T(8,128)(2,1)} %reshape.226, bf16[1,3584,128]{2,1,0:T(8,128)(2,1)} %collective-permute-done.2, bf16[1,3584,128]{2,1,0:T(8,128)(2,1)} %param.13, pred[]{:T(512)S(6)} %eq.85), kind=kOutput, calls=%fused_computation.15 | convolution fusion | flops 1409744896 | bytes 13631489 | tf_op jit(solution)/shard_map/dot_general | solution.py:85
  646.1 5.7 multiply_reduce_fusion
  651.8 4.0 fusion.7
  655.9 4.3 fusion.6
  660.2 0.1 reshape.230
  660.3 44.8 %psum.7 = f32[256,6]{1,0:T(8,128)S(1)} all-reduce(f32[256,6]{1,0:T(8,128)S(1)} %reshape.230), channel_id=1, replica_groups=mesh['dp'=8,'expert'=32] {'dp'}, use_global_device_ids=true, to_apply=%region_7.8 | all-reduce | flops 1536 | bytes 12288 | tf_op jit(solution)/shard_map/psum | solution.py:103
  705.1 0.6 constant_dynamic-slice_fusion
  705.7 47.3 %all-to-all-start.3 = ((f32[32,1,6]{2,1,0:T(1,128)}), f32[32,1,6]{2,1,0:T(1,128)S(1)}, u32[]{:S(2)}, u32[]{:S(2)}) async-start(f32[32,1,6]{2,1,0:T(1,128)} %bitcast.11), calls=%async_computation.3 | async-start | bytes 32768 | tf_op jit(solution)/shard_map/all_to_all | solution.py:105
  753.1 6.9 fusion.8
  760.0 0.4 all-to-all-done.3
  760.4 0.5 broadcast.262
  760.9 0.7 reduce.4
  761.7 6.8 gather_fusion.3
  768.7 0.6 compare_select_fusion.4
  (58 shorter events, 1.2 us)
Async XLA Ops:
  27.2 52.7 %all-to-all-start = ((bf16[32,6,3584]{2,1,0:T(8,128)(2,1)}), bf16[32,6,3584]{2,1,0:T(8,128)(2,1)S(1)}, u32[]{:S(2)}, u32[]{:S(2)}) async-start(bf16[32,6,3584]{2,1,0:T(8,128)(2,1)} %reshape.224), calls=%async_computation | async-start | bytes 3670016 | tf_op jit(solution)/shard_map/all_to_all | solution.py:66
  37.4 521.7 %all-gather.3.cloned.1.call-start = ((), (), s32[]{:S(2)}) async-start(), calls=%async_computation.4 | async-start | bytes 24772608 | tf_op jit(solution)/shard_map/all_gather | solution.py:11
  41.2 93.2 %copy-start = (bf16[1,3584,128]{2,1,0:T(8,128)(2,1)S(1)}, bf16[1,3584,128]{2,1,0:T(8,128)(2,1)}, u32[]{:S(2)}) copy-start(bf16[1,3584,128]{2,1,0:T(8,128)(2,1)} %param.14) | copy-start | bytes 2752516
  41.2 96.6 %copy-start.2 = (bf16[128,8]{0,1:T(8,128)(2,1)S(1)}, bf16[128,8]{0,1:T(8,128)(2,1)}, u32[]{:S(2)}) copy-start(bf16[128,8]{0,1:T(8,128)(2,1)} %param.11) | copy-start | bytes 6148
  44.7 101.6 %copy-start.3 = (s32[16]{0:T(128)S(1)}, s32[16]{0:T(128)}, u32[]{:S(2)}) copy-start(s32[16]{0:T(128)} %param.12) | copy-start | bytes 196
  134.4 495.3 %collective-permute-start.1 = (bf16[1,3584,128]{2,1,0:T(8,128)(2,1)S(1)}, bf16[1,3584,128]{2,1,0:T(8,128)(2,1)S(1)}, u32[]{:S(2)}, u32[]{:S(2)}) collective-permute-start(bf16[1,3584,128]{2,1,0:T(8,128)(2,1)S(1)} %copy-done), channel_id=1, source_target_pairs={{0,16},{16,0},{1,17},{17,1},{2,18},{18,2},{3,19},{19,3},{4,20},{20... | collective-permute-start | bytes 2752520 | tf_op jit(solution)/shard_map/ppermute | solution.py:25
  135.4 502.4 %collective-permute-start.2 = (bf16[1,3584,128]{2,1,0:T(8,128)(2,1)}, bf16[1,3584,128]{2,1,0:T(8,128)(2,1)}, u32[]{:S(2)}, u32[]{:S(2)}) collective-permute-start(bf16[1,3584,128]{2,1,0:T(8,128)(2,1)} %param.13), channel_id=1, source_target_pairs={{0,16},{16,0},{1,17},{17,1},{2,18},{18,2},{3,19},{19,3},{4,20},{20... | collective-permute-start | bytes 2752520 | tf_op jit(solution)/shard_map/ppermute | solution.py:25
  136.9 509.2 %collective-permute-start = (bf16[1,128,3584]{2,1,0:T(8,128)(2,1)}, bf16[1,128,3584]{2,1,0:T(8,128)(2,1)}, u32[]{:S(2)}, u32[]{:S(2)}) collective-permute-start(bf16[1,128,3584]{2,1,0:T(8,128)(2,1)} %param.15), channel_id=1, source_target_pairs={{0,16},{16,0},{1,17},{17,1},{2,18},{18,2},{3,19},{19,3},{4,20},{20... | collective-permute-start | bytes 2752520 | tf_op jit(solution)/shard_map/ppermute | solution.py:25
  140.4 295.0 %all-to-all-start.2 = ((bf16[32,1,6]{2,1,0:T(2,128)(2,1)}), bf16[32,1,6]{2,1,0:T(2,128)(2,1)S(1)}, u32[]{:S(2)}, u32[]{:S(2)}) async-start(bf16[32,1,6]{2,1,0:T(2,128)(2,1)} %all_to_all.27), calls=%async_computation.2 | async-start | bytes 32768 | tf_op jit(solution)/shard_map/all_to_all | solution.py:68
  629.8 16.3 %slice-start.3 = ((s8[11010048]{0:T(1024)(128)(4,1)}), s8[4194304]{0:T(1024)(128)(4,1)S(1)}, s32[]{:S(2)}) async-start(s8[11010048]{0:T(1024)(128)(4,1)} %bitcast.45), calls=%async_computation.8 | async-start | bytes 8388608
  629.8 16.3 %slice-start.4 = ((s8[11010048]{0:T(1024)(128)(4,1)}), s8[4194304]{0:T(1024)(128)(4,1)S(1)}, s32[]{:S(2)}) async-start(s8[11010048]{0:T(1024)(128)(4,1)} %bitcast.45), calls=%async_computation.9 | async-start | bytes 8388608
  637.8 8.3 %slice-start.5 = ((s8[11010048]{0:T(1024)(128)(4,1)}), s8[2621440]{0:T(1024)(128)(4,1)S(1)}, s32[]{:S(2)}) async-start(s8[11010048]{0:T(1024)(128)(4,1)} %bitcast.45), calls=%async_computation.10 | async-start | bytes 5242880
  637.8 14.0 %slice-start = ((s8[11010048]{0:T(1024)(128)(4,1)}), s8[4194304]{0:T(1024)(128)(4,1)S(1)}, s32[]{:S(2)}) async-start(s8[11010048]{0:T(1024)(128)(4,1)} %bitcast.43), calls=%async_computation.5 | async-start | bytes 8388608
  637.8 14.0 %slice-start.1 = ((s8[11010048]{0:T(1024)(128)(4,1)}), s8[2621440]{0:T(1024)(128)(4,1)S(1)}, s32[]{:S(2)}) async-start(s8[11010048]{0:T(1024)(128)(4,1)} %bitcast.43), calls=%async_computation.6 | async-start | bytes 5242880
  646.1 5.8 slice-start.2
  655.9 97.2 %copy-start.4 = (bf16[1536,128]{0,1:T(8,128)(2,1)S(1)}, bf16[1536,128]{0,1:T(8,128)(2,1)}, u32[]{:S(2)}) copy-start(bf16[1536,128]{0,1:T(8,128)(2,1)} %get-tuple-element.23) | copy-start | bytes 1179652
  660.2 108.5 %copy-start.1 = (s32[128,8]{0,1:T(8,128)S(1)}, s32[128,8]{0,1:T(8,128)}, u32[]{:S(2)}) copy-start(s32[128,8]{0,1:T(8,128)} %param.10) | copy-start | bytes 12292
  705.7 54.7 %all-to-all-start.3 = ((f32[32,1,6]{2,1,0:T(1,128)}), f32[32,1,6]{2,1,0:T(1,128)S(1)}, u32[]{:S(2)}, u32[]{:S(2)}) async-start(f32[32,1,6]{2,1,0:T(1,128)} %bitcast.11), calls=%async_computation.3 | async-start | bytes 32768 | tf_op jit(solution)/shard_map/all_to_all | solution.py:105
Sparse Core Ops, SparseCore 0:
  134.5 300.4 all-gather.2
